TPU v7x, 512 devices: a whole 4x4x16 slice. The times are simulated.
512 devices in a mesh: seq: 64 (over z_lo, y, core), tp: 8 (over z_hi, x).
Axes of the slice: x: 4, y: 4, z: 16 (z_hi: 2, z_lo: 8; z = z_hi * 8 + z_lo), core: 2. Of those that a mesh axis runs over, the one named last changes fastest.
Arguments:
- queries: bfloat16 [16384, 2048], P('seq', 'tp'), may hold values from -42 to 42
- keys: bfloat16 [16384, 2048], P('seq', 'tp'), may hold values from -6.1 to 6.1
- values: bfloat16 [16384, 2048], P('seq', 'tp'), may hold values from -6 to 6
- residual_in: bfloat16 [16384, 2048], P('seq', 'tp'), may hold values from -6 to 6
- bias_table: float32 [16, 32], P('tp'), may hold values from -4 to 4
- buckets: int32 [128, 33], P('seq'), may hold values from 0 to 31
- out_weight: bfloat16 [2048, 2048], P('tp'), may hold values from -0.125 to 0.125
- gate_weight: bfloat16 [2048, 4096], P('seq', 'tp'), may hold values from -0.125 to 0.125
- up_weight: bfloat16 [2048, 4096], P('seq', 'tp'), may hold values from -0.125 to 0.125
- down_weight_t: bfloat16 [2048, 4096], P('seq', 'tp'), may hold values from -0.09375 to 0.09375
- norm_gain: float32 [2048], replicated, may hold values from 0.5 to 1.5
Outputs:
- layer_out: bfloat16 [16384, 2048], P('seq', 'tp')
All inputs are finite; a program needn't handle non-finite values.
Results may differ from a plain program's by a relative error of at most 0.015.
Values may be sent and summed in bfloat16 or wider, within the bound.
A program may use at most 64 MiB of HBM per device.

v0:
```python
import jax
import jax.numpy as jnp
from jax import lax
from jax.sharding import PartitionSpec as P

HEAD_DIM = 128
BUCKETS = 32
TILE = 128
HALF_BAND = 2048
OFFSETS = 33


def shifted(x, axis, by):
    devices = lax.axis_size(axis)
    pairs = [(i, i + by) for i in range(devices) if 0 <= i + by < devices]
    return lax.ppermute(x, axis, pairs)


def attend_local(queries, extended, bucket_blk, table, start, total_len, width):
    rows = queries.shape[0]
    heads = table.shape[0]
    span = rows + 2 * width
    q3 = queries.reshape(rows, heads, HEAD_DIM)
    k3 = extended[0].reshape(span, heads, HEAD_DIM)
    v3 = extended[1].reshape(span, heads, HEAD_DIM)
    scores = jnp.einsum("qhd,khd->hqk", q3, k3, preferred_element_type=jnp.float32) * HEAD_DIM ** (
        -0.5
    )
    tiles_q = rows // TILE
    tiles_k = span // TILE
    onehot = (bucket_blk[:, :, None] == jnp.arange(BUCKETS, dtype=jnp.int32)[None, None, :]).astype(
        jnp.float32
    )
    table_vals = jnp.einsum("qob,hb->hqo", onehot, table, precision=lax.Precision.HIGHEST)
    offset = (
        jnp.arange(tiles_k, dtype=jnp.int32)[None, :]
        - jnp.arange(tiles_q, dtype=jnp.int32)[:, None]
    )
    select = (offset[:, :, None] == jnp.arange(OFFSETS, dtype=jnp.int32)[None, None, :]).astype(
        jnp.float32
    )
    tile_bias = jnp.einsum("qko,hqo->hqk", select, table_vals, precision=lax.Precision.HIGHEST)
    scores = scores.reshape(heads, tiles_q, TILE, tiles_k, TILE) + tile_bias[:, :, None, :, None]
    scores = scores.reshape(heads, rows, span)
    qpos = start + jnp.arange(rows, dtype=jnp.int32)[:, None]
    kpos = start - width + jnp.arange(span, dtype=jnp.int32)[None, :]
    valid = (jnp.abs(qpos - kpos) <= width) & (kpos >= 0) & (kpos < total_len)
    masked = jnp.where(valid[None], scores, -1e30)
    top = jnp.max(masked, axis=-1, keepdims=True)
    expo = jnp.where(valid[None], jnp.exp(masked - top), 0.0)
    weight = (expo / jnp.sum(expo, axis=-1, keepdims=True)).astype(jnp.bfloat16)
    out = jnp.einsum("hqk,khd->qhd", weight, v3, preferred_element_type=jnp.float32)
    return out.astype(jnp.bfloat16).reshape(rows, heads * HEAD_DIM)


def normalize(full_state, norm_gain):
    wide = full_state.astype(jnp.float32)
    scale = lax.rsqrt(jnp.mean(wide * wide, axis=-1, keepdims=True) + 1e-05)
    return (wide * scale * norm_gain).astype(jnp.bfloat16)


def shards(
    queries,
    keys,
    values,
    residual_in,
    bias_table,
    buckets,
    out_weight,
    gate_weight,
    up_weight,
    down_weight_t,
    norm_gain,
):
    rows = queries.shape[0]
    width = HALF_BAND
    reach = width // rows
    paired = jnp.stack([keys, values], 0)
    offsets_list = list(range(reach, 0, -1)) + list(range(-1, -reach - 1, -1))
    arrived = []
    for distance in offsets_list:
        arrived.append(shifted(paired, "seq", distance))
    extended = jnp.concatenate(arrived[:reach] + [paired] + arrived[reach:], axis=1)
    start = lax.axis_index("seq") * rows
    total_len = rows * lax.axis_size("seq")
    attended = attend_local(queries, extended, buckets, bias_table, start, total_len, width)
    partial_value = jnp.dot(attended, out_weight, preferred_element_type=jnp.float32)
    own_sum = lax.psum_scatter(
        partial_value.astype(jnp.bfloat16), "tp", scatter_dimension=1, tiled=True
    ).astype(jnp.float32)
    own_state = (residual_in.astype(jnp.float32) + own_sum).astype(jnp.bfloat16)
    full_state = lax.all_gather(own_state, "tp", axis=1, tiled=True)
    normed = normalize(full_state, norm_gain)
    gate_all, up_all, down_all = (
        lax.all_gather(gate_weight, "seq", axis=0, tiled=True),
        lax.all_gather(up_weight, "seq", axis=0, tiled=True),
        lax.all_gather(down_weight_t, "seq", axis=0, tiled=True),
    )
    gate = jnp.dot(normed, gate_all, preferred_element_type=jnp.float32)
    up = jnp.dot(normed, up_all, preferred_element_type=jnp.float32)
    hidden = (jax.nn.silu(gate) * up).astype(jnp.bfloat16)
    terms = lax.dot_general(
        hidden, down_all, (((1,), (1,)), ((), ())), preferred_element_type=jnp.float32
    )
    ffn_own = lax.psum_scatter(
        terms.astype(jnp.bfloat16), "tp", scatter_dimension=1, tiled=True
    ).astype(jnp.float32)
    return (own_state.astype(jnp.float32) + ffn_own).astype(jnp.bfloat16)


def solution(mesh):
    return jax.shard_map(
        shards,
        mesh=mesh,
        in_specs=(
            P("seq", "tp"),
            P("seq", "tp"),
            P("seq", "tp"),
            P("seq", "tp"),
            P("tp", None),
            P("seq", None),
            P("tp", None),
            P("seq", "tp"),
            P("seq", "tp"),
            P("seq", "tp"),
            P(),
        ),
        out_specs=P("seq", "tp"),
        check_vma=False,
    )
```

profile of v0, /device:TPU:8, one launch (start us, length us, event | category | flops | bytes accessed | tf_op | source)
XLA Modules:
  0.0 815.9 jit_solution(12422391377847241001)
XLA Ops:
  6.5 1.1 copy.16
  7.6 1.0 copy.17
  8.7 4.5 collective-permute-start
  13.2 2.9 collective-permute-start.1
  16.1 4.2 collective-permute-start.2
  20.3 3.7 collective-permute-start.3
  24.0 5.4 collective-permute-start.4
  29.5 0.9 convolution_bitcast_fusion
  30.4 3.7 fusion.4
  34.2 0.2 convolution_bitcast_fusion.1
  34.4 0.1 copy.20
  34.5 5.9 add.69
  40.3 12.3 %add.70 = f32[2,256,4352]{1,2,0:T(8,128)} reshape(f32[2,2,128,34,128]{2,1,4,3,0:T(2,128)} %add.69) | data formatting | bytes 17825792 | tf_op jit(solution)/shard_map/add | solution.py:43
  52.6 2.6 collective-permute-start.5
  55.3 1.0 constant_dynamic-update-slice_fusion.16
  56.3 0.0 collective-permute-done.1
  56.3 4.1 collective-permute-start.6
  60.4 1.0 constant_dynamic-update-slice_fusion.15
  61.3 3.3 collective-permute-start.7
  64.7 2.3 collective-permute-start.8
  67.0 1.9 collective-permute-start.9
  69.0 1.3 collective-permute-start.10
  70.3 1.3 collective-permute-start.11
  71.6 1.3 collective-permute-start.12
  73.0 1.3 collective-permute-start.13
  74.3 5.8 collective-permute-done.9
  80.2 1.3 collective-permute-start.14
  81.5 1.6 collective-permute-done.10
  83.1 1.3 collective-permute-start.15
  84.4 7.0 collective-permute-done.11
  91.4 1.8 collective-permute-done.12
  93.2 17.2 %collective-permute-done.13 = bf16[2,256,256]{1,2,0:T(8,128)(2,1)S(1)} collective-permute-done((bf16[2,256,256]{1,2,0:T(8,128)(2,1)S(1)}, bf16[2,256,256]{1,2,0:T(8,128)(2,1)S(1)}, u32[]{:S(2)}, u32[]{:S(2)}) %collective-permute-start.13) | collective-permute-done | bytes 262176 | tf_op jit(solution)/shard_map/ppermute | solution.py:16
  110.4 3.8 collective-permute-done.14
  114.2 4.0 collective-permute-done.15
  118.3 1.6 fusion.29
  120.0 2.7 copy-done.1
  122.7 2.0 fusion.2
  124.7 5.8 fusion.30
  130.5 4.4 fusion.10
  134.9 0.0 copy-start.7
  135.0 1.5 convolution_convert_fusion.1
  136.4 0.0 reduce-scatter.3.cloned.1.call-update
  136.4 0.2 all-gather.5.cloned.1.call-start
  136.7 117.1 %reduce-scatter.3.cloned.1.call-done = bf16[256,256]{1,0:T(8,128)(2,1)} async-done(((bf16[256,2048]{1,0:T(8,128)(2,1)}), bf16[256,256]{1,0:T(8,128)(2,1)}) %reduce-scatter.3.cloned.1.call-update) | async-done | bytes 131088 | tf_op jit(solution)/shard_map/reduce_scatter | solution.py:88
  253.8 1.6 add_convert_fusion.1
  255.4 0.0 all-gather.5.cloned.1.call-update
  255.4 0.0 all-gather.7.cloned.1.call-start
  255.5 0.7 all-gather.7.cloned.1.call-update
  256.1 0.0 all-gather.11.cloned.1.call-start
  256.2 0.5 all-gather.11.cloned.1.call-update
  256.7 0.0 all-gather.9.cloned.1.call-start
  256.8 0.5 all-gather.9.cloned.1.call-update
  257.3 0.0 reduce-scatter.5.cloned.1.call-start
  257.4 79.4 %all-gather.5.cloned.1.call-done = bf16[256,2048]{1,0:T(8,128)(2,1)} async-done(((bf16[256,256]{1,0:T(8,128)(2,1)}), bf16[256,2048]{1,0:T(8,128)(2,1)}) %all-gather.5.cloned.1.call-update) | async-done | bytes 1048592 | tf_op jit(solution)/shard_map/all_gather | solution.py:92
  336.7 1.6 fusion.6
  338.3 111.6 %all-gather.7.cloned.1.call-done = bf16[2048,512]{1,0:T(8,128)(2,1)} async-done(((bf16[32,512]{1,0:T(8,128)(2,1)}), bf16[2048,512]{1,0:T(8,128)(2,1)}) %all-gather.7.cloned.1.call-update) | async-done | bytes 2097168 | tf_op jit(solution)/shard_map/all_gather | solution.py:95
  450.0 2.7 fusion.18
  452.7 0.0 copy-start.3
  452.7 116.1 %all-gather.11.cloned.1.call-done = bf16[2048,512]{1,0:T(8,128)(2,1)} async-done(((bf16[32,512]{1,0:T(8,128)(2,1)}), bf16[2048,512]{1,0:T(8,128)(2,1)}) %all-gather.11.cloned.1.call-update) | async-done | bytes 2097168 | tf_op jit(solution)/shard_map/all_gather | solution.py:97
  568.7 118.8 %all-gather.9.cloned.1.call-done = bf16[2048,512]{1,0:T(8,128)(2,1)} async-done(((bf16[32,512]{1,0:T(8,128)(2,1)}), bf16[2048,512]{1,0:T(8,128)(2,1)}) %all-gather.9.cloned.1.call-update) | async-done | bytes 2097168 | tf_op jit(solution)/shard_map/all_gather | solution.py:96
  687.5 4.6 convolution_convert_fusion
  692.2 0.0 reduce-scatter.5.cloned.1.call-update
  692.2 115.3 %reduce-scatter.5.cloned.1.call-done = bf16[256,256]{1,0:T(8,128)(2,1)} async-done(((bf16[256,2048]{1,0:T(8,128)(2,1)}), bf16[256,256]{1,0:T(8,128)(2,1)}) %reduce-scatter.5.cloned.1.call-update) | async-done | bytes 131088 | tf_op jit(solution)/shard_map/reduce_scatter | solution.py:105
  807.5 1.6 add_convert_fusion
  (43 shorter events, 0.4 us)
Async XLA Ops:
  6.5 128.4 %copy-start = (bf16[256,2048]{1,0:T(8,128)(2,1)S(1)}, bf16[256,2048]{1,0:T(8,128)(2,1)}, u32[]{:S(2)}) copy-start(bf16[256,2048]{1,0:T(8,128)(2,1)} %param.17) | copy-start | bytes 3145732
  6.5 247.3 %reduce-scatter.3.cloned.1.call-start = ((), (), s32[]{:S(2)}) async-start(), calls=%async_computation.2 | async-start | bytes 1179648 | tf_op jit(solution)/shard_map/reduce_scatter | solution.py:88
  8.7 44.0 %collective-permute-start = (bf16[2,256,256]{1,2,0:T(8,128)(2,1)S(1)}, bf16[2,256,256]{1,2,0:T(8,128)(2,1)}, u32[]{:S(2)}, u32[]{:S(2)}) collective-permute-start(bf16[2,256,256]{1,2,0:T(8,128)(2,1)S(1)} %pad_maximum_fusion), channel_id=1, source_target_pairs={{0,64},{8,72},{16,80},{24,88},{32,96},{40,104},{48,112},{56,120},{... | collective-permute-start | bytes 786440 | tf_op jit(solution)/shard_map/ppermute | solution.py:16
  13.2 43.0 %collective-permute-start.1 = (bf16[2,256,256]{1,2,0:T(8,128)(2,1)S(1)}, bf16[2,256,256]{1,2,0:T(8,128)(2,1)}, u32[]{:S(2)}, u32[]{:S(2)}) collective-permute-start(bf16[2,256,256]{1,2,0:T(8,128)(2,1)S(1)} %pad_maximum_fusion), channel_id=1, source_target_pairs={{0,56},{8,64},{16,72},{24,80},{32,88},{40,96},{48,104},{56,112},{6... | collective-permute-start | bytes 786440 | tf_op jit(solution)/shard_map/ppermute | solution.py:16
  16.1 45.2 %collective-permute-start.2 = (bf16[2,256,256]{1,2,0:T(8,128)(2,1)S(1)}, bf16[2,256,256]{1,2,0:T(8,128)(2,1)S(1)}, u32[]{:S(2)}, u32[]{:S(2)}) collective-permute-start(bf16[2,256,256]{1,2,0:T(8,128)(2,1)S(1)} %pad_maximum_fusion), channel_id=1, source_target_pairs={{0,48},{8,56},{16,64},{24,72},{32,80},{40,88},{48,96},{56,104},{64... | collective-permute-start | bytes 786440 | tf_op jit(solution)/shard_map/ppermute | solution.py:16
  20.3 44.3 %collective-permute-start.3 = (bf16[2,256,256]{1,2,0:T(8,128)(2,1)S(1)}, bf16[2,256,256]{1,2,0:T(8,128)(2,1)S(1)}, u32[]{:S(2)}, u32[]{:S(2)}) collective-permute-start(bf16[2,256,256]{1,2,0:T(8,128)(2,1)S(1)} %pad_maximum_fusion), channel_id=1, source_target_pairs={{0,40},{8,48},{16,56},{24,64},{32,72},{40,80},{48,88},{56,96},{64,... | collective-permute-start | bytes 786440 | tf_op jit(solution)/shard_map/ppermute | solution.py:16
  24.0 43.0 %collective-permute-start.4 = (bf16[2,256,256]{1,2,0:T(8,128)(2,1)S(1)}, bf16[2,256,256]{1,2,0:T(8,128)(2,1)S(1)}, u32[]{:S(2)}, u32[]{:S(2)}) collective-permute-start(bf16[2,256,256]{1,2,0:T(8,128)(2,1)S(1)} %pad_maximum_fusion), channel_id=1, source_target_pairs={{0,32},{8,40},{16,48},{24,56},{32,64},{40,72},{48,80},{56,88},{64,... | collective-permute-start | bytes 786440 | tf_op jit(solution)/shard_map/ppermute | solution.py:16
  52.6 16.3 %collective-permute-start.5 = (bf16[2,256,256]{1,2,0:T(8,128)(2,1)S(1)}, bf16[2,256,256]{1,2,0:T(8,128)(2,1)S(1)}, u32[]{:S(2)}, u32[]{:S(2)}) collective-permute-start(bf16[2,256,256]{1,2,0:T(8,128)(2,1)S(1)} %pad_maximum_fusion), channel_id=1, source_target_pairs={{0,24},{8,32},{16,40},{24,48},{32,56},{40,64},{48,72},{56,80},{64,... | collective-permute-start | bytes 786440 | tf_op jit(solution)/shard_map/ppermute | solution.py:16
  56.3 14.0 %collective-permute-start.6 = (bf16[2,256,256]{1,2,0:T(8,128)(2,1)S(1)}, bf16[2,256,256]{1,2,0:T(8,128)(2,1)S(1)}, u32[]{:S(2)}, u32[]{:S(2)}) collective-permute-start(bf16[2,256,256]{1,2,0:T(8,128)(2,1)S(1)} %pad_maximum_fusion), channel_id=1, source_target_pairs={{0,16},{8,24},{16,32},{24,40},{32,48},{40,56},{48,64},{56,72},{64,... | collective-permute-start | bytes 786440 | tf_op jit(solution)/shard_map/ppermute | solution.py:16
  61.3 10.3 %collective-permute-start.7 = (bf16[2,256,256]{1,2,0:T(8,128)(2,1)S(1)}, bf16[2,256,256]{1,2,0:T(8,128)(2,1)S(1)}, u32[]{:S(2)}, u32[]{:S(2)}) collective-permute-start(bf16[2,256,256]{1,2,0:T(8,128)(2,1)S(1)} %pad_maximum_fusion), channel_id=1, source_target_pairs={{0,8},{8,16},{16,24},{24,32},{32,40},{40,48},{48,56},{56,64},{64,7... | collective-permute-start | bytes 786440 | tf_op jit(solution)/shard_map/ppermute | solution.py:16
  64.7 8.3 %collective-permute-start.8 = (bf16[2,256,256]{1,2,0:T(8,128)(2,1)S(1)}, bf16[2,256,256]{1,2,0:T(8,128)(2,1)S(1)}, u32[]{:S(2)}, u32[]{:S(2)}) collective-permute-start(bf16[2,256,256]{1,2,0:T(8,128)(2,1)S(1)} %pad_maximum_fusion), channel_id=1, source_target_pairs={{8,0},{16,8},{24,16},{32,24},{40,32},{48,40},{56,48},{64,56},{72,6... | collective-permute-start | bytes 786440 | tf_op jit(solution)/shard_map/ppermute | solution.py:16
  67.0 13.2 %collective-permute-start.9 = (bf16[2,256,256]{1,2,0:T(8,128)(2,1)S(1)}, bf16[2,256,256]{1,2,0:T(8,128)(2,1)S(1)}, u32[]{:S(2)}, u32[]{:S(2)}) collective-permute-start(bf16[2,256,256]{1,2,0:T(8,128)(2,1)S(1)} %pad_maximum_fusion), channel_id=1, source_target_pairs={{16,0},{24,8},{32,16},{40,24},{48,32},{56,40},{64,48},{72,56},{80,... | collective-permute-start | bytes 786440 | tf_op jit(solution)/shard_map/ppermute | solution.py:16
  69.0 14.1 %collective-permute-start.10 = (bf16[2,256,256]{1,2,0:T(8,128)(2,1)S(1)}, bf16[2,256,256]{1,2,0:T(8,128)(2,1)S(1)}, u32[]{:S(2)}, u32[]{:S(2)}) collective-permute-start(bf16[2,256,256]{1,2,0:T(8,128)(2,1)S(1)} %pad_maximum_fusion), channel_id=1, source_target_pairs={{24,0},{32,8},{40,16},{48,24},{56,32},{64,40},{72,48},{80,56},{88,... | collective-permute-start | bytes 786440 | tf_op jit(solution)/shard_map/ppermute | solution.py:16
  70.3 21.1 %collective-permute-start.11 = (bf16[2,256,256]{1,2,0:T(8,128)(2,1)S(1)}, bf16[2,256,256]{1,2,0:T(8,128)(2,1)S(1)}, u32[]{:S(2)}, u32[]{:S(2)}) collective-permute-start(bf16[2,256,256]{1,2,0:T(8,128)(2,1)S(1)} %pad_maximum_fusion), channel_id=1, source_target_pairs={{32,0},{40,8},{48,16},{56,24},{64,32},{72,40},{80,48},{88,56},{96,... | collective-permute-start | bytes 786440 | tf_op jit(solution)/shard_map/ppermute | solution.py:16
  71.6 21.6 %collective-permute-start.12 = (bf16[2,256,256]{1,2,0:T(8,128)(2,1)S(1)}, bf16[2,256,256]{1,2,0:T(8,128)(2,1)S(1)}, u32[]{:S(2)}, u32[]{:S(2)}) collective-permute-start(bf16[2,256,256]{1,2,0:T(8,128)(2,1)S(1)} %pad_maximum_fusion), channel_id=1, source_target_pairs={{40,0},{48,8},{56,16},{64,24},{72,32},{80,40},{88,48},{96,56},{104... | collective-permute-start | bytes 786440 | tf_op jit(solution)/shard_map/ppermute | solution.py:16
  73.0 37.4 %collective-permute-start.13 = (bf16[2,256,256]{1,2,0:T(8,128)(2,1)S(1)}, bf16[2,256,256]{1,2,0:T(8,128)(2,1)S(1)}, u32[]{:S(2)}, u32[]{:S(2)}) collective-permute-start(bf16[2,256,256]{1,2,0:T(8,128)(2,1)S(1)} %pad_maximum_fusion), channel_id=1, source_target_pairs={{48,0},{56,8},{64,16},{72,24},{80,32},{88,40},{96,48},{104,56},{11... | collective-permute-start | bytes 786440 | tf_op jit(solution)/shard_map/ppermute | solution.py:16
  80.2 34.0 %collective-permute-start.14 = (bf16[2,256,256]{1,2,0:T(8,128)(2,1)S(1)}, bf16[2,256,256]{1,2,0:T(8,128)(2,1)S(1)}, u32[]{:S(2)}, u32[]{:S(2)}) collective-permute-start(bf16[2,256,256]{1,2,0:T(8,128)(2,1)S(1)} %pad_maximum_fusion), channel_id=1, source_target_pairs={{56,0},{64,8},{72,16},{80,24},{88,32},{96,40},{104,48},{112,56},{1... | collective-permute-start | bytes 786440 | tf_op jit(solution)/shard_map/ppermute | solution.py:16
  83.1 35.2 %collective-permute-start.15 = (bf16[2,256,256]{1,2,0:T(8,128)(2,1)S(1)}, bf16[2,256,256]{1,2,0:T(8,128)(2,1)S(1)}, u32[]{:S(2)}, u32[]{:S(2)}) collective-permute-start(bf16[2,256,256]{1,2,0:T(8,128)(2,1)S(1)} %pad_maximum_fusion), channel_id=1, source_target_pairs={{64,0},{72,8},{80,16},{88,24},{96,32},{104,40},{112,48},{120,56},{... | collective-permute-start | bytes 786440 | tf_op jit(solution)/shard_map/ppermute | solution.py:16
  118.3 1.7 copy-start.5
  118.3 4.4 copy-start.1
  124.7 5.8 copy-start.2
  130.5 123.3 %copy-start.6 = (bf16[256,256]{1,0:T(8,128)(2,1)S(1)}, bf16[256,256]{1,0:T(8,128)(2,1)}, u32[]{:S(2)}) copy-start(bf16[256,256]{1,0:T(8,128)(2,1)} %param.14) | copy-start | bytes 393220
  134.9 315.0 %copy-start.7 = (f32[2048]{0:T(1024)S(1)}, f32[2048]{0:T(1024)}, u32[]{:S(2)}) copy-start(f32[2048]{0:T(1024)} %param.21) | copy-start | bytes 24580
  136.4 200.3 %all-gather.5.cloned.1.call-start = ((), (), s32[]{:S(2)}) async-start(), calls=%async_computation.3 | async-start | bytes 1179648 | tf_op jit(solution)/shard_map/all_gather | solution.py:92
  255.4 194.6 %all-gather.7.cloned.1.call-start = ((), (), s32[]{:S(2)}) async-start(), calls=%async_computation.4 | async-start | bytes 2129920 | tf_op jit(solution)/shard_map/all_gather | solution.py:95
  256.1 312.6 %all-gather.11.cloned.1.call-start = ((), (), s32[]{:S(2)}) async-start(), calls=%async_computation.6 | async-start | bytes 2129920 | tf_op jit(solution)/shard_map/all_gather | solution.py:97
  256.7 430.8 %all-gather.9.cloned.1.call-start = ((), (), s32[]{:S(2)}) async-start(), calls=%async_computation.5 | async-start | bytes 2129920 | tf_op jit(solution)/shard_map/all_gather | solution.py:96
  257.3 550.2 %reduce-scatter.5.cloned.1.call-start = ((), (), s32[]{:S(2)}) async-start(), calls=%async_computation.7 | async-start | bytes 1179648 | tf_op jit(solution)/shard_map/reduce_scatter | solution.py:105
  336.7 350.8 %copy-start.4 = (bf16[256,2048]{1,0:T(8,128)(2,1)S(1)}, bf16[256,2048]{1,0:T(8,128)(2,1)}, u32[]{:S(2)}) copy-start(bf16[256,2048]{1,0:T(8,128)(2,1)} %all-gather.5.cloned.1.call-done) | copy-start | bytes 3145732
  452.7 354.8 %copy-start.3 = (bf16[256,256]{1,0:T(8,128)(2,1)S(1)}, bf16[256,256]{1,0:T(8,128)(2,1)}, u32[]{:S(2)}) copy-start(bf16[256,256]{1,0:T(8,128)(2,1)} %add_convert_fusion.1) | copy-start | bytes 393220
Sparse Core Ops, SparseCore 0:
  136.6 117.1 reduce-scatter.2
  257.3 79.3 all-gather.4
  339.1 110.8 all-gather.6
  452.2 116.4 all-gather.10
  571.0 116.4 all-gather.8
  692.6 114.9 reduce-scatter.4
where the time goes:
time: 817 us; the launch traced here: 816 us
  waiting for transfers between devices  701 us (86%)
  starting transfers between devices  43 us (5%)
  local copies, waits for them, and re-layouts  27 us (3%)
  matrix products  16.3 us (2%)
  other arithmetic  14.4 us (2%)
  between operations  13.9 us (2%)
    all_gather x1, waiting for transfers between devices, shards(): lax.all_gather(up_weight, 'seq', axis=0, tiled=True)  119 us
    reduce_scatter x1, waiting for transfers between devices, shards(): lax.psum_scatter(partial_value.astype(jnp.bfloat16), 'tp', scatter_dimens...  117 us
    all_gather x1, waiting for transfers between devices, shards(): lax.all_gather(down_weight_t, 'seq', axis=0, tiled=True)  116 us
    reduce_scatter x1, waiting for transfers between devices, shards(): lax.psum_scatter(terms.astype(jnp.bfloat16), 'tp', scatter_dimension=1, t...  115 us
    all_gather x1, waiting for transfers between devices, shards(): lax.all_gather(gate_weight, 'seq', axis=0, tiled=True)  112 us
    all_gather x1, waiting for transfers between devices, shards(): full_state = lax.all_gather(own_state, 'tp', axis=1, tiled=True)  79.4 us
    ppermute x16, starting transfers between devices, shifted(): return lax.ppermute(x, axis, pairs)  42.7 us
    ppermute x16, waiting for transfers between devices, shifted(): return lax.ppermute(x, axis, pairs)  41.2 us
  transfers between devices with their start and end apart: 22, of which 13 were waited for; matrix products, arithmetic and copies ran while one was open for 4% of the time, Pallas kernels for 0%

commit v1 on v0

--- a/solution.py
+++ b/solution.py
@@ -89,7 +89,9 @@
         partial_value.astype(jnp.bfloat16), "tp", scatter_dimension=1, tiled=True
     ).astype(jnp.float32)
     own_state = (residual_in.astype(jnp.float32) + own_sum).astype(jnp.bfloat16)
-    full_state = lax.all_gather(own_state, "tp", axis=1, tiled=True)
+    full_state = jnp.concatenate(
+        lax.all_to_all(jnp.stack([own_state] * lax.axis_size("tp")), "tp", 0, 0), axis=1
+    )
     normed = normalize(full_state, norm_gain)
     gate_all, up_all, down_all = (
         lax.all_gather(gate_weight, "seq", axis=0, tiled=True),

time: 817 us -> 673 us (0.82)
  waiting for transfers between devices: 701 us -> 553 us
    all_gather x1, waiting for transfers between devices: 112 us -> 0.03 us  [shards(): lax.all_gather(gate_weight, 'seq', axis=0, tiled=True)]
    all_gather x1 -> x0, waiting for transfers between devices: 79.4 us -> none  [shards(): full_state = lax.all_gather(own_state, 'tp', axis=1, tiled=True)]
    all_to_all x0 -> x1, waiting for transfers between devices: none -> 25.2 us  [shards(): lax.all_to_all(jnp.stack([own_state] * lax.axis_size('tp')), 'tp', 0, 0)]
    all_gather x1, waiting for transfers between devices: 119 us -> 134 us  [shards(): lax.all_gather(up_weight, 'seq', axis=0, tiled=True)]
  transfers between devices with their start and end apart: 22 -> 22, of which waited for: 13 -> 12; matrix products, arithmetic and copies ran while one was open for 4% -> 5% of each run, Pallas kernels for 0% -> 0%
where the time goes in v1:
time: 673 us; the launch traced here: 672 us
  waiting for transfers between devices  553 us (82%)
  starting transfers between devices  46.7 us (7%)
  local copies, waits for them, and re-layouts  28.1 us (4%)
  matrix products  15.9 us (2%)
  between operations  15.5 us (2%)
  other arithmetic  12.8 us (2%)
    all_gather x1, waiting for transfers between devices, shards(): lax.all_gather(up_weight, 'seq', axis=0, tiled=True)  134 us
    all_gather x1, waiting for transfers between devices, shards(): lax.all_gather(down_weight_t, 'seq', axis=0, tiled=True)  119 us
    reduce_scatter x1, waiting for transfers between devices, shards(): lax.psum_scatter(partial_value.astype(jnp.bfloat16), 'tp', scatter_dimens...  117 us
    reduce_scatter x1, waiting for transfers between devices, shards(): lax.psum_scatter(terms.astype(jnp.bfloat16), 'tp', scatter_dimension=1, t...  115 us
    ppermute x16, starting transfers between devices, shifted(): return lax.ppermute(x, axis, pairs)  42.7 us
    ppermute x16, waiting for transfers between devices, shifted(): return lax.ppermute(x, axis, pairs)  41.2 us
    all_to_all x1, waiting for transfers between devices, shards(): lax.all_to_all(jnp.stack([own_state] * lax.axis_size('tp')), 'tp', 0, 0)  25.2 us
    add x2, local copies, waits for them, and re-layouts, attend_local(): scores.reshape(heads, tiles_q, TILE, tiles_k, TILE)  18.2 us
  transfers between devices with their start and end apart: 22, of which 12 were waited for; matrix products, arithmetic and copies ran while one was open for 5% of the time, Pallas kernels for 0%

profile of v1, /device:TPU:8, one launch (start us, length us, event | category | flops | bytes accessed | tf_op | source)
XLA Modules:
  0.0 672.1 jit_solution(17352176545157547694)
XLA Ops:
  7.4 1.1 copy.16
  8.5 1.0 copy.17
  9.5 4.5 collective-permute-start
  14.0 2.9 collective-permute-start.1
  16.9 4.2 collective-permute-start.2
  21.2 3.7 collective-permute-start.3
  24.9 5.4 collective-permute-start.4
  30.3 0.9 convolution_bitcast_fusion
  31.2 3.7 fusion.4
  35.0 0.2 convolution_bitcast_fusion.1
  35.2 0.1 copy.20
  35.3 5.9 add.69
  41.2 12.3 %add.70 = f32[2,256,4352]{1,2,0:T(8,128)} reshape(f32[2,2,128,34,128]{2,1,4,3,0:T(2,128)} %add.69) | data formatting | bytes 17825792 | tf_op jit(solution)/shard_map/add | solution.py:43
  53.5 2.6 collective-permute-start.5
  56.1 1.0 constant_dynamic-update-slice_fusion.16
  57.1 4.1 collective-permute-start.6
  61.2 1.0 constant_dynamic-update-slice_fusion.15
  62.2 3.3 collective-permute-start.7
  65.5 2.3 collective-permute-start.8
  67.8 1.9 collective-permute-start.9
  69.8 1.3 collective-permute-start.10
  71.1 1.3 collective-permute-start.11
  72.5 1.3 collective-permute-start.12
  73.8 1.3 collective-permute-start.13
  75.2 5.8 collective-permute-done.9
  81.0 1.3 collective-permute-start.14
  82.3 1.6 collective-permute-done.10
  83.9 1.3 collective-permute-start.15
  85.2 7.0 %collective-permute-done.11 = bf16[2,256,256]{1,2,0:T(8,128)(2,1)S(1)} collective-permute-done((bf16[2,256,256]{1,2,0:T(8,128)(2,1)S(1)}, bf16[2,256,256]{1,2,0:T(8,128)(2,1)S(1)}, u32[]{:S(2)}, u32[]{:S(2)}) %collective-permute-start.11) | collective-permute-done | bytes 262176 | tf_op jit(solution)/shard_map/ppermute | solution.py:16
  92.2 1.8 collective-permute-done.12
  94.0 17.2 %collective-permute-done.13 = bf16[2,256,256]{1,2,0:T(8,128)(2,1)S(1)} collective-permute-done((bf16[2,256,256]{1,2,0:T(8,128)(2,1)S(1)}, bf16[2,256,256]{1,2,0:T(8,128)(2,1)S(1)}, u32[]{:S(2)}, u32[]{:S(2)}) %collective-permute-start.13) | collective-permute-done | bytes 262176 | tf_op jit(solution)/shard_map/ppermute | solution.py:16
  111.2 3.8 collective-permute-done.14
  115.1 4.0 collective-permute-done.15
  119.1 1.6 fusion.24
  120.8 2.7 copy-done.1
  123.5 2.0 fusion.2
  125.5 5.8 fusion.25
  131.3 4.4 fusion.9
  135.8 0.0 copy-start.5
  135.8 1.5 convolution_convert_fusion.1
  137.3 0.0 reduce-scatter.3.cloned.1.call-update
  137.3 0.0 all-gather.4.cloned.1.call-start
  137.3 0.5 all-gather.4.cloned.1.call-update
  137.9 0.2 all-gather.6.cloned.1.call-start
  138.1 0.4 all-gather.6.cloned.1.call-update
  138.4 116.7 %reduce-scatter.3.cloned.1.call-done = bf16[256,256]{1,0:T(8,128)(2,1)} async-done(((bf16[256,2048]{1,0:T(8,128)(2,1)}), bf16[256,256]{1,0:T(8,128)(2,1)}) %reduce-scatter.3.cloned.1.call-update) | async-done | bytes 131088 | tf_op jit(solution)/shard_map/reduce_scatter | solution.py:88
  255.1 0.9 add_convert_fusion.1
  256.1 0.1 copy.22
  256.2 1.0 stack.11
  257.2 3.7 all-to-all-start
  260.9 0.0 all-gather.8.cloned.1.call-start
  261.0 0.5 all-gather.8.cloned.1.call-update
  261.5 0.0 reduce-scatter.5.cloned.1.call-start
  261.5 25.2 %all-to-all-done = bf16[8,256,256]{1,2,0:T(8,128)(2,1)S(1)} async-done(((bf16[8,256,256]{1,2,0:T(8,128)(2,1)}), bf16[8,256,256]{1,2,0:T(8,128)(2,1)S(1)}, u32[]{:S(2)}, u32[]{:S(2)}) %all-to-all-start) | async-done | bytes 1048608 | tf_op jit(solution)/shard_map/all_to_all | solution.py:93
  286.8 0.3 multiply_reduce_fusion
  287.1 0.3 fusion.7
  287.4 0.0 all-gather.4.cloned.1.call-done
  287.5 2.3 fusion.26
  289.8 134.4 %all-gather.6.cloned.1.call-done = bf16[2048,512]{1,0:T(8,128)(2,1)} async-done(((bf16[32,512]{1,0:T(8,128)(2,1)}), bf16[2048,512]{1,0:T(8,128)(2,1)}) %all-gather.6.cloned.1.call-update) | async-done | bytes 2097168 | tf_op jit(solution)/shard_map/all_gather | solution.py:98
  424.2 119.0 %all-gather.8.cloned.1.call-done = bf16[2048,512]{1,0:T(8,128)(2,1)} async-done(((bf16[32,512]{1,0:T(8,128)(2,1)}), bf16[2048,512]{1,0:T(8,128)(2,1)}) %all-gather.8.cloned.1.call-update) | async-done | bytes 2097168 | tf_op jit(solution)/shard_map/all_gather | solution.py:99
  543.3 4.6 convolution_convert_fusion
  547.8 0.0 reduce-scatter.5.cloned.1.call-update
  547.9 115.0 %reduce-scatter.5.cloned.1.call-done = bf16[256,256]{1,0:T(8,128)(2,1)} async-done(((bf16[256,2048]{1,0:T(8,128)(2,1)}), bf16[256,256]{1,0:T(8,128)(2,1)}) %reduce-scatter.5.cloned.1.call-update) | async-done | bytes 131088 | tf_op jit(solution)/shard_map/reduce_scatter | solution.py:107
  662.9 1.6 add_convert_fusion
  (41 shorter events, 0.4 us)
Async XLA Ops:
  7.4 128.4 %copy-start = (bf16[256,2048]{1,0:T(8,128)(2,1)S(1)}, bf16[256,2048]{1,0:T(8,128)(2,1)}, u32[]{:S(2)}) copy-start(bf16[256,2048]{1,0:T(8,128)(2,1)} %param.17) | copy-start | bytes 3145732
  7.4 247.8 %reduce-scatter.3.cloned.1.call-start = ((), (), s32[]{:S(2)}) async-start(), calls=%async_computation.3 | async-start | bytes 1179648 | tf_op jit(solution)/shard_map/reduce_scatter | solution.py:88
  9.5 44.0 %collective-permute-start = (bf16[2,256,256]{1,2,0:T(8,128)(2,1)S(1)}, bf16[2,256,256]{1,2,0:T(8,128)(2,1)}, u32[]{:S(2)}, u32[]{:S(2)}) collective-permute-start(bf16[2,256,256]{1,2,0:T(8,128)(2,1)S(1)} %pad_maximum_fusion), channel_id=1, source_target_pairs={{0,64},{8,72},{16,80},{24,88},{32,96},{40,104},{48,112},{56,120},{... | collective-permute-start | bytes 786440 | tf_op jit(solution)/shard_map/ppermute | solution.py:16
  14.0 43.1 %collective-permute-start.1 = (bf16[2,256,256]{1,2,0:T(8,128)(2,1)S(1)}, bf16[2,256,256]{1,2,0:T(8,128)(2,1)}, u32[]{:S(2)}, u32[]{:S(2)}) collective-permute-start(bf16[2,256,256]{1,2,0:T(8,128)(2,1)S(1)} %pad_maximum_fusion), channel_id=1, source_target_pairs={{0,56},{8,64},{16,72},{24,80},{32,88},{40,96},{48,104},{56,112},{6... | collective-permute-start | bytes 786440 | tf_op jit(solution)/shard_map/ppermute | solution.py:16
  16.9 45.2 %collective-permute-start.2 = (bf16[2,256,256]{1,2,0:T(8,128)(2,1)S(1)}, bf16[2,256,256]{1,2,0:T(8,128)(2,1)S(1)}, u32[]{:S(2)}, u32[]{:S(2)}) collective-permute-start(bf16[2,256,256]{1,2,0:T(8,128)(2,1)S(1)} %pad_maximum_fusion), channel_id=1, source_target_pairs={{0,48},{8,56},{16,64},{24,72},{32,80},{40,88},{48,96},{56,104},{64... | collective-permute-start | bytes 786440 | tf_op jit(solution)/shard_map/ppermute | solution.py:16
  21.2 44.3 %collective-permute-start.3 = (bf16[2,256,256]{1,2,0:T(8,128)(2,1)S(1)}, bf16[2,256,256]{1,2,0:T(8,128)(2,1)S(1)}, u32[]{:S(2)}, u32[]{:S(2)}) collective-permute-start(bf16[2,256,256]{1,2,0:T(8,128)(2,1)S(1)} %pad_maximum_fusion), channel_id=1, source_target_pairs={{0,40},{8,48},{16,56},{24,64},{32,72},{40,80},{48,88},{56,96},{64,... | collective-permute-start | bytes 786440 | tf_op jit(solution)/shard_map/ppermute | solution.py:16
  24.9 43.0 %collective-permute-start.4 = (bf16[2,256,256]{1,2,0:T(8,128)(2,1)S(1)}, bf16[2,256,256]{1,2,0:T(8,128)(2,1)S(1)}, u32[]{:S(2)}, u32[]{:S(2)}) collective-permute-start(bf16[2,256,256]{1,2,0:T(8,128)(2,1)S(1)} %pad_maximum_fusion), channel_id=1, source_target_pairs={{0,32},{8,40},{16,48},{24,56},{32,64},{40,72},{48,80},{56,88},{64,... | collective-permute-start | bytes 786440 | tf_op jit(solution)/shard_map/ppermute | solution.py:16
  53.5 16.3 %collective-permute-start.5 = (bf16[2,256,256]{1,2,0:T(8,128)(2,1)S(1)}, bf16[2,256,256]{1,2,0:T(8,128)(2,1)S(1)}, u32[]{:S(2)}, u32[]{:S(2)}) collective-permute-start(bf16[2,256,256]{1,2,0:T(8,128)(2,1)S(1)} %pad_maximum_fusion), channel_id=1, source_target_pairs={{0,24},{8,32},{16,40},{24,48},{32,56},{40,64},{48,72},{56,80},{64,... | collective-permute-start | bytes 786440 | tf_op jit(solution)/shard_map/ppermute | solution.py:16
  57.1 14.0 %collective-permute-start.6 = (bf16[2,256,256]{1,2,0:T(8,128)(2,1)S(1)}, bf16[2,256,256]{1,2,0:T(8,128)(2,1)S(1)}, u32[]{:S(2)}, u32[]{:S(2)}) collective-permute-start(bf16[2,256,256]{1,2,0:T(8,128)(2,1)S(1)} %pad_maximum_fusion), channel_id=1, source_target_pairs={{0,16},{8,24},{16,32},{24,40},{32,48},{40,56},{48,64},{56,72},{64,... | collective-permute-start | bytes 786440 | tf_op jit(solution)/shard_map/ppermute | solution.py:16
  62.2 10.3 %collective-permute-start.7 = (bf16[2,256,256]{1,2,0:T(8,128)(2,1)S(1)}, bf16[2,256,256]{1,2,0:T(8,128)(2,1)S(1)}, u32[]{:S(2)}, u32[]{:S(2)}) collective-permute-start(bf16[2,256,256]{1,2,0:T(8,128)(2,1)S(1)} %pad_maximum_fusion), channel_id=1, source_target_pairs={{0,8},{8,16},{16,24},{24,32},{32,40},{40,48},{48,56},{56,64},{64,7... | collective-permute-start | bytes 786440 | tf_op jit(solution)/shard_map/ppermute | solution.py:16
  65.5 8.3 %collective-permute-start.8 = (bf16[2,256,256]{1,2,0:T(8,128)(2,1)S(1)}, bf16[2,256,256]{1,2,0:T(8,128)(2,1)S(1)}, u32[]{:S(2)}, u32[]{:S(2)}) collective-permute-start(bf16[2,256,256]{1,2,0:T(8,128)(2,1)S(1)} %pad_maximum_fusion), channel_id=1, source_target_pairs={{8,0},{16,8},{24,16},{32,24},{40,32},{48,40},{56,48},{64,56},{72,6... | collective-permute-start | bytes 786440 | tf_op jit(solution)/shard_map/ppermute | solution.py:16
  67.8 13.2 %collective-permute-start.9 = (bf16[2,256,256]{1,2,0:T(8,128)(2,1)S(1)}, bf16[2,256,256]{1,2,0:T(8,128)(2,1)S(1)}, u32[]{:S(2)}, u32[]{:S(2)}) collective-permute-start(bf16[2,256,256]{1,2,0:T(8,128)(2,1)S(1)} %pad_maximum_fusion), channel_id=1, source_target_pairs={{16,0},{24,8},{32,16},{40,24},{48,32},{56,40},{64,48},{72,56},{80,... | collective-permute-start | bytes 786440 | tf_op jit(solution)/shard_map/ppermute | solution.py:16
  69.8 14.1 %collective-permute-start.10 = (bf16[2,256,256]{1,2,0:T(8,128)(2,1)S(1)}, bf16[2,256,256]{1,2,0:T(8,128)(2,1)S(1)}, u32[]{:S(2)}, u32[]{:S(2)}) collective-permute-start(bf16[2,256,256]{1,2,0:T(8,128)(2,1)S(1)} %pad_maximum_fusion), channel_id=1, source_target_pairs={{24,0},{32,8},{40,16},{48,24},{56,32},{64,40},{72,48},{80,56},{88,... | collective-permute-start | bytes 786440 | tf_op jit(solution)/shard_map/ppermute | solution.py:16
  71.1 21.1 %collective-permute-start.11 = (bf16[2,256,256]{1,2,0:T(8,128)(2,1)S(1)}, bf16[2,256,256]{1,2,0:T(8,128)(2,1)S(1)}, u32[]{:S(2)}, u32[]{:S(2)}) collective-permute-start(bf16[2,256,256]{1,2,0:T(8,128)(2,1)S(1)} %pad_maximum_fusion), channel_id=1, source_target_pairs={{32,0},{40,8},{48,16},{56,24},{64,32},{72,40},{80,48},{88,56},{96,... | collective-permute-start | bytes 786440 | tf_op jit(solution)/shard_map/ppermute | solution.py:16
  72.5 21.6 %collective-permute-start.12 = (bf16[2,256,256]{1,2,0:T(8,128)(2,1)S(1)}, bf16[2,256,256]{1,2,0:T(8,128)(2,1)S(1)}, u32[]{:S(2)}, u32[]{:S(2)}) collective-permute-start(bf16[2,256,256]{1,2,0:T(8,128)(2,1)S(1)} %pad_maximum_fusion), channel_id=1, source_target_pairs={{40,0},{48,8},{56,16},{64,24},{72,32},{80,40},{88,48},{96,56},{104... | collective-permute-start | bytes 786440 | tf_op jit(solution)/shard_map/ppermute | solution.py:16
  73.8 37.4 %collective-permute-start.13 = (bf16[2,256,256]{1,2,0:T(8,128)(2,1)S(1)}, bf16[2,256,256]{1,2,0:T(8,128)(2,1)S(1)}, u32[]{:S(2)}, u32[]{:S(2)}) collective-permute-start(bf16[2,256,256]{1,2,0:T(8,128)(2,1)S(1)} %pad_maximum_fusion), channel_id=1, source_target_pairs={{48,0},{56,8},{64,16},{72,24},{80,32},{88,40},{96,48},{104,56},{11... | collective-permute-start | bytes 786440 | tf_op jit(solution)/shard_map/ppermute | solution.py:16
  81.0 34.0 %collective-permute-start.14 = (bf16[2,256,256]{1,2,0:T(8,128)(2,1)S(1)}, bf16[2,256,256]{1,2,0:T(8,128)(2,1)S(1)}, u32[]{:S(2)}, u32[]{:S(2)}) collective-permute-start(bf16[2,256,256]{1,2,0:T(8,128)(2,1)S(1)} %pad_maximum_fusion), channel_id=1, source_target_pairs={{56,0},{64,8},{72,16},{80,24},{88,32},{96,40},{104,48},{112,56},{1... | collective-permute-start | bytes 786440 | tf_op jit(solution)/shard_map/ppermute | solution.py:16
  83.9 35.2 %collective-permute-start.15 = (bf16[2,256,256]{1,2,0:T(8,128)(2,1)S(1)}, bf16[2,256,256]{1,2,0:T(8,128)(2,1)S(1)}, u32[]{:S(2)}, u32[]{:S(2)}) collective-permute-start(bf16[2,256,256]{1,2,0:T(8,128)(2,1)S(1)} %pad_maximum_fusion), channel_id=1, source_target_pairs={{64,0},{72,8},{80,16},{88,24},{96,32},{104,40},{112,48},{120,56},{... | collective-permute-start | bytes 786440 | tf_op jit(solution)/shard_map/ppermute | solution.py:16
  119.1 1.7 copy-start.3
  119.1 4.4 copy-start.1
  125.5 5.8 copy-start.2
  131.3 123.8 %copy-start.4 = (bf16[256,256]{1,0:T(8,128)(2,1)S(1)}, bf16[256,256]{1,0:T(8,128)(2,1)}, u32[]{:S(2)}) copy-start(bf16[256,256]{1,0:T(8,128)(2,1)} %param.14) | copy-start | bytes 393220
  135.8 151.3 %copy-start.5 = (f32[2048]{0:T(1024)S(1)}, f32[2048]{0:T(1024)}, u32[]{:S(2)}) copy-start(f32[2048]{0:T(1024)} %param.21) | copy-start | bytes 24580
  137.3 150.2 %all-gather.4.cloned.1.call-start = ((), (), s32[]{:S(2)}) async-start(), calls=%async_computation.4 | async-start | bytes 2129920 | tf_op jit(solution)/shard_map/all_gather | solution.py:97
  137.9 286.3 %all-gather.6.cloned.1.call-start = ((), (), s32[]{:S(2)}) async-start(), calls=%async_computation.5 | async-start | bytes 2129920 | tf_op jit(solution)/shard_map/all_gather | solution.py:98
  257.2 29.6 %all-to-all-start = ((bf16[8,256,256]{1,2,0:T(8,128)(2,1)}), bf16[8,256,256]{1,2,0:T(8,128)(2,1)S(1)}, u32[]{:S(2)}, u32[]{:S(2)}) async-start(bf16[8,256,256]{1,2,0:T(8,128)(2,1)} %stack.11), calls=%async_computation.1 | async-start | bytes 2097152 | tf_op jit(solution)/shard_map/all_to_all | solution.py:93
  260.9 282.3 %all-gather.8.cloned.1.call-start = ((), (), s32[]{:S(2)}) async-start(), calls=%async_computation.6 | async-start | bytes 2129920 | tf_op jit(solution)/shard_map/all_gather | solution.py:99
  261.5 401.4 %reduce-scatter.5.cloned.1.call-start = ((), (), s32[]{:S(2)}) async-start(), calls=%async_computation.7 | async-start | bytes 1179648 | tf_op jit(solution)/shard_map/reduce_scatter | solution.py:107
Sparse Core Ops, SparseCore 0:
  137.4 117.6 reduce-scatter.2
  548.0 114.8 reduce-scatter.4
Sparse Core Ops, SparseCore 1:
  140.1 131.9 all-gather.3
  274.4 149.8 all-gather.5
  426.5 116.7 all-gather.7
